TPU v7x, 32 devices: a whole 2x2x4 slice. The times are simulated.
32 devices in a mesh: dp: 8 (over z, y), tensor: 4 (over x, core).
Axes of the slice: x: 2, y: 2, z: 4, core: 2. Of those that a mesh axis runs over, the one named last changes fastest.
Arguments:
- tokens: bfloat16 [8192, 1024], P(('dp', 'tensor')), may hold values from -6 to 6
- cotangent: bfloat16 [8192, 1024], P(('dp', 'tensor')), may hold values from -6 to 6
- prefix: int32 [8], P('dp'), may hold values from 102 to 512
- qkv_weight: float32 [1024, 3, 1024], P('dp', None, 'tensor'), may hold values from -0.1875 to 0.1875
- qkv_moment: float32 [1024, 3, 1024], P('dp', None, 'tensor'), may hold values from -112 to 112
- qkv_square: float32 [1024, 3, 1024], P('dp', None, 'tensor'), may hold values from 24.576 to 2457.6
- out_weight: float32 [1024, 1024], P('dp', 'tensor'), may hold values from -1 to 1
- out_moment: float32 [1024, 1024], P('dp', 'tensor'), may hold values from -112 to 112
- out_square: float32 [1024, 1024], P('dp', 'tensor'), may hold values from 24.576 to 2457.6
- up_weight: float32 [1024, 4096], P('dp', 'tensor'), may hold values from -0.1875 to 0.1875
- up_moment: float32 [1024, 4096], P('dp', 'tensor'), may hold values from -112 to 112
- up_square: float32 [1024, 4096], P('dp', 'tensor'), may hold values from 24.576 to 2457.6
- down_weight: float32 [1024, 4096], P('dp', 'tensor'), may hold values from -0.09375 to 0.09375
- down_moment: float32 [1024, 4096], P('dp', 'tensor'), may hold values from -112 to 112
- down_square: float32 [1024, 4096], P('dp', 'tensor'), may hold values from 24.576 to 2457.6
- norm_gains: float32 [2, 1024], replicated, may hold values from 0.5 to 1.5
- gains_moment: float32 [2, 1024], replicated, may hold values from -256 to 256
- gains_square: float32 [2, 1024], replicated, may hold values from 245.76 to 8192
- biases: float32 [6, 1024], replicated, may hold values from -1.75 to 1.75
- biases_moment: float32 [6, 1024], replicated, may hold values from -256 to 256
- biases_square: float32 [6, 1024], replicated, may hold values from 8192 to 819200
- up_bias: float32 [4096], replicated, may hold values from -1.75 to 1.75
- up_bias_moment: float32 [4096], replicated, may hold values from -256 to 256
- up_bias_square: float32 [4096], replicated, may hold values from 245.76 to 8192
Outputs:
- output: bfloat16 [8192, 1024], P(('dp', 'tensor'))
- input_grad: float32 [8192, 1024], P(('dp', 'tensor'))
- qkv_weight_grad: float32 [1024, 3, 1024], P('dp', None, 'tensor')
- out_weight_grad: float32 [1024, 1024], P('dp', 'tensor')
- up_weight_grad: float32 [1024, 4096], P('dp', 'tensor')
- down_weight_grad: float32 [1024, 4096], P('dp', 'tensor')
- norm_gains_grad: float32 [2, 1024], replicated
- biases_grad: float32 [6, 1024], replicated
- up_bias_grad: float32 [4096], replicated
- qkv_weight_new: float32 [1024, 3, 1024], P('dp', None, 'tensor')
- out_weight_new: float32 [1024, 1024], P('dp', 'tensor')
- up_weight_new: float32 [1024, 4096], P('dp', 'tensor')
- down_weight_new: float32 [1024, 4096], P('dp', 'tensor')
- norm_gains_new: float32 [2, 1024], replicated
- biases_new: float32 [6, 1024], replicated
- up_bias_new: float32 [4096], replicated
- qkv_weight_low: bfloat16 [1024, 3, 1024], P('dp', None, 'tensor')
- out_weight_low: bfloat16 [1024, 1024], P('dp', 'tensor')
- up_weight_low: bfloat16 [1024, 4096], P('dp', 'tensor')
- down_weight_low: bfloat16 [1024, 4096], P('dp', 'tensor')
- qkv_moment_new: float32 [1024, 3, 1024], P('dp', None, 'tensor')
- out_moment_new: float32 [1024, 1024], P('dp', 'tensor')
- up_moment_new: float32 [1024, 4096], P('dp', 'tensor')
- down_moment_new: float32 [1024, 4096], P('dp', 'tensor')
- gains_moment_new: float32 [2, 1024], replicated
- biases_moment_new: float32 [6, 1024], replicated
- up_bias_moment_new: float32 [4096], replicated
- qkv_square_new: float32 [1024, 3, 1024], P('dp', None, 'tensor')
- out_square_new: float32 [1024, 1024], P('dp', 'tensor')
- up_square_new: float32 [1024, 4096], P('dp', 'tensor')
- down_square_new: float32 [1024, 4096], P('dp', 'tensor')
- gains_square_new: float32 [2, 1024], replicated
- biases_square_new: float32 [6, 1024], replicated
- up_bias_square_new: float32 [4096], replicated
- weight_norms: float32 [4], replicated
- step_norms: float32 [4], replicated
All inputs are finite; a program needn't handle non-finite values.
Results may differ from a plain program's by a relative error of at most 0.022.
Values may be sent and summed in bfloat16 or wider, within the bound.
No kernel may reach another device: no remote copies, remote signals or barrier semaphores. Data moves between devices by JAX's collectives and lax.ppermute only.
A program may use at most 128 MiB of HBM per device.

v0:
```python
import jax
import jax.numpy as jnp
from jax import lax
from jax.sharding import PartitionSpec as P

HEADS = 16
HEAD = 64
QBLOCK = 512
learn_rate = 0.5
gelu_coef = 0.7978845608028654


def norm_forward(values, gain, shift):
    mean = jnp.mean(values, axis=-1, keepdims=True)
    centred = values - mean
    inverse = lax.rsqrt(jnp.mean(centred * centred, axis=-1, keepdims=True) + 1e-05)
    unit = centred * inverse
    return (unit * gain + shift, unit, inverse)


def norm_backward(grad, unit, inverse, gain):
    scaled = grad * gain
    inner = (
        scaled
        - jnp.mean(scaled, axis=-1, keepdims=True)
        - unit * jnp.mean(scaled * unit, axis=-1, keepdims=True)
    )
    return (inverse * inner, jnp.sum(grad * unit, axis=0), jnp.sum(grad, axis=0))


def gelu_value(v):
    return 0.5 * v * (1.0 + jnp.tanh(gelu_coef * (v + 0.044715 * v * v * v)))


def gelu_slope(v):
    hyper = jnp.tanh(gelu_coef * (v + 0.044715 * v * v * v))
    return 0.5 * (1.0 + hyper) + 0.5 * v * (1.0 - hyper * hyper) * gelu_coef * (
        1.0 + 3.0 * 0.044715 * v * v
    )


def alibi_slopes():
    return jnp.exp2(-8.0 * (lax.iota(jnp.int32, HEADS) + 1).astype(jnp.float32) / HEADS)


def block_scores(queries, keys, slope, start, prefix_len, scale):
    count = queries.shape[0]
    length = keys.shape[0]
    scores = jnp.einsum("bhe,khe->hbk", queries, keys, preferred_element_type=jnp.float32) * scale
    row_pos = start + lax.iota(jnp.int32, count)
    col_pos = lax.iota(jnp.int32, length)
    offset = (col_pos[None, :] - row_pos[:, None]).astype(jnp.float32)
    scores = scores + slope[:, None, None] * offset[None]
    allowed = (col_pos[None, :] <= row_pos[:, None]) | (col_pos[None, :] < prefix_len)
    return (scores, allowed)


def place(part, width, rank):
    return lax.dynamic_update_slice(jnp.zeros((width,), jnp.float32), part, (rank * part.shape[0],))


def adam_terms(moment, square, grad):
    new_moment = 0.5 * moment + 0.5 * grad
    new_square = 0.5 * square + 0.5 * grad * grad
    return (new_moment, new_square, new_moment / (jnp.sqrt(new_square) + 1e-06))


def lamb_rows(weight, moment, square, grad):
    new_moment, new_square, direction = adam_terms(moment, square, grad)
    weight_norm = jnp.sqrt(jnp.sum(weight * weight, axis=-1, keepdims=True))
    step_norm = jnp.sqrt(jnp.sum(direction * direction, axis=-1, keepdims=True))
    return (weight - learn_rate * (weight_norm / step_norm) * direction, new_moment, new_square)


def per_device(
    tokens,
    cotangent,
    prefix,
    qkv_weight,
    qkv_moment,
    qkv_square,
    out_weight,
    out_moment,
    out_square,
    up_weight,
    up_moment,
    up_square,
    down_weight,
    down_moment,
    down_square,
    norm_gains,
    gains_moment,
    gains_square,
    biases,
    biases_moment,
    biases_square,
    up_bias,
    up_bias_moment,
    up_bias_square,
):
    rows = tokens.shape[0]
    length = rows * lax.axis_size("tensor")
    rank = lax.axis_index("tensor")
    local_width = qkv_weight.shape[2]
    local_hidden = up_weight.shape[1]
    heads_here = local_width // HEAD
    block = min(QBLOCK, length)
    blocks = length // block
    scale = float(HEAD) ** (-0.5)
    prefix_len = prefix[0]
    slope = lax.dynamic_slice_in_dim(alibi_slopes(), rank * heads_here, heads_here)
    shards = (
        qkv_weight.astype(jnp.bfloat16),
        out_weight.astype(jnp.bfloat16),
        up_weight.astype(jnp.bfloat16),
        down_weight.astype(jnp.bfloat16),
    )
    qkv_full, out_full, up_full, down_full = (
        lax.all_gather(shards[0], "dp", axis=0, tiled=True),
        lax.all_gather(shards[1], "dp", axis=0, tiled=True),
        lax.all_gather(shards[2], "dp", axis=0, tiled=True),
        lax.all_gather(shards[3], "dp", axis=0, tiled=True),
    )
    x_rows = tokens.astype(jnp.float32)
    normed, unit_one, inverse_one = norm_forward(x_rows, norm_gains[0], biases[0])
    normed_all = lax.all_gather(normed.astype(jnp.bfloat16), "tensor", axis=0, tiled=True)
    projected = jnp.einsum("ld,dce->cle", normed_all, qkv_full, preferred_element_type=jnp.float32)
    query_bias = lax.dynamic_slice_in_dim(biases[2], rank * local_width, local_width)
    value_bias = lax.dynamic_slice_in_dim(biases[3], rank * local_width, local_width)
    query_heads = (projected[0] + query_bias).astype(jnp.bfloat16).reshape(length, heads_here, HEAD)
    key_heads = projected[1].astype(jnp.bfloat16).reshape(length, heads_here, HEAD)
    value_heads = (projected[2] + value_bias).astype(jnp.bfloat16).reshape(length, heads_here, HEAD)

    def attend(block_index):
        start = block_index * block
        queries = lax.dynamic_slice_in_dim(query_heads, start, block, 0)
        scores, allowed = block_scores(queries, key_heads, slope, start, prefix_len, scale)
        scores = jnp.where(allowed[None], scores, -1e30)
        peak = jnp.max(scores, axis=-1, keepdims=True)
        expo = jnp.exp(scores - peak)
        totals = jnp.sum(expo, axis=-1, keepdims=True)
        probs = (expo / totals).astype(jnp.bfloat16)
        mixed = jnp.einsum("hbk,khe->bhe", probs, value_heads, preferred_element_type=jnp.float32)
        return (mixed.reshape(block, local_width), (peak + jnp.log(totals))[..., 0])

    mixed, logsum = lax.map(attend, lax.iota(jnp.int32, blocks))
    context_low = mixed.reshape(length, local_width).astype(jnp.bfloat16)
    piece = context_low
    attn_rows = lax.psum_scatter(
        jnp.einsum("le,de->ld", piece, out_full, preferred_element_type=jnp.float32),
        "tensor",
        scatter_dimension=0,
        tiled=True,
    )
    resid = x_rows + (attn_rows + biases[4])
    normed_two, unit_two, inverse_two = norm_forward(resid, norm_gains[1], biases[1])
    normed_two_low = normed_two.astype(jnp.bfloat16)
    normed_two_all = lax.all_gather(normed_two_low, "tensor", axis=0, tiled=True)
    up_slice = lax.dynamic_slice_in_dim(up_bias, rank * local_hidden, local_hidden)
    pre = jnp.dot(normed_two_all, up_full, preferred_element_type=jnp.float32) + up_slice
    hidden_low = gelu_value(pre).astype(jnp.bfloat16)
    piece = hidden_low
    mlp_rows = lax.psum_scatter(
        jnp.einsum("lf,df->ld", piece, down_full, preferred_element_type=jnp.float32).astype(
            jnp.bfloat16
        ),
        "tensor",
        scatter_dimension=0,
        tiled=True,
    ).astype(jnp.float32)
    output = (resid + (mlp_rows + biases[5])).astype(jnp.bfloat16)
    qkv_full, out_full, up_full, down_full = (
        lax.all_gather(shards[0], "dp", axis=0, tiled=True),
        lax.all_gather(shards[1], "dp", axis=0, tiled=True),
        lax.all_gather(shards[2], "dp", axis=0, tiled=True),
        lax.all_gather(shards[3], "dp", axis=0, tiled=True),
    )
    out_grad = cotangent.astype(jnp.float32)
    down_bias_part = jnp.sum(out_grad, axis=0)
    mlp_grad_all = lax.all_gather(cotangent, "tensor", axis=0, tiled=True)
    down_grad = jnp.einsum(
        "ld,lf->df", mlp_grad_all, hidden_low, preferred_element_type=jnp.float32
    )
    hidden_grad = jnp.dot(mlp_grad_all, down_full, preferred_element_type=jnp.float32)
    pre_grad = (hidden_grad * gelu_slope(pre)).astype(jnp.bfloat16)
    up_bias_part = place(jnp.sum(pre_grad, axis=0, dtype=jnp.float32), up_bias.shape[0], rank)
    up_grad = jnp.einsum("ld,lf->df", normed_two_all, pre_grad, preferred_element_type=jnp.float32)
    piece = pre_grad
    normed_two_grad = lax.psum_scatter(
        jnp.einsum("lf,df->ld", piece, up_full, preferred_element_type=jnp.float32),
        "tensor",
        scatter_dimension=0,
        tiled=True,
    )
    resid_from_norm, gain_two_part, shift_two_part = norm_backward(
        normed_two_grad, unit_two, inverse_two, norm_gains[1]
    )
    resid_grad = out_grad + resid_from_norm
    branch_low = resid_grad.astype(jnp.bfloat16)
    out_bias_part = jnp.sum(branch_low, axis=0, dtype=jnp.float32)
    branch_all = lax.all_gather(branch_low, "tensor", axis=0, tiled=True)
    out_weight_part = jnp.einsum(
        "ld,le->de", branch_all, context_low, preferred_element_type=jnp.float32
    )
    context_grad = jnp.dot(branch_all, out_full, preferred_element_type=jnp.float32).astype(
        jnp.bfloat16
    )
    grad_heads = context_grad.reshape(length, heads_here, HEAD)

    def attend_back(carry, block_index):
        key_grad, value_grad = carry
        start = block_index * block
        queries = lax.dynamic_slice_in_dim(query_heads, start, block, 0)
        grad_out = lax.dynamic_slice_in_dim(grad_heads, start, block, 0)
        scores, allowed = block_scores(queries, key_heads, slope, start, prefix_len, scale)
        probs = jnp.where(allowed[None], jnp.exp(scores - logsum[block_index][..., None]), 0.0)
        prob_grad = jnp.einsum(
            "bhe,khe->hbk", grad_out, value_heads, preferred_element_type=jnp.float32
        )
        delta = jnp.sum(probs * prob_grad, axis=-1, keepdims=True)
        score_grad = (probs * (prob_grad - delta)).astype(jnp.bfloat16)
        query_grad = (
            jnp.einsum("hbk,khe->bhe", score_grad, key_heads, preferred_element_type=jnp.float32)
            * scale
        )
        key_grad = (
            key_grad
            + jnp.einsum("hbk,bhe->khe", score_grad, queries, preferred_element_type=jnp.float32)
            * scale
        )
        value_grad = value_grad + jnp.einsum(
            "hbk,bhe->khe", probs.astype(jnp.bfloat16), grad_out, preferred_element_type=jnp.float32
        )
        return ((key_grad, value_grad), query_grad.reshape(block, local_width))

    empty = jnp.zeros((length, heads_here, HEAD), jnp.float32)
    (key_grad, value_grad), query_grad = lax.scan(
        attend_back, (empty, empty), lax.iota(jnp.int32, blocks)
    )
    query_low = query_grad.reshape(length, local_width).astype(jnp.bfloat16)
    key_low = key_grad.reshape(length, local_width).astype(jnp.bfloat16)
    value_low = value_grad.reshape(length, local_width).astype(jnp.bfloat16)
    stacked_grad = jnp.stack([query_low, key_low, value_low])
    qkv_part = jnp.einsum(
        "ld,cle->dce", normed_all, stacked_grad, preferred_element_type=jnp.float32
    )
    piece = stacked_grad
    normed_grad = lax.psum_scatter(
        jnp.einsum("cle,dce->ld", piece, qkv_full, preferred_element_type=jnp.float32).astype(
            jnp.bfloat16
        ),
        "tensor",
        scatter_dimension=0,
        tiled=True,
    ).astype(jnp.float32)
    input_from_norm, gain_one_part, shift_one_part = norm_backward(
        normed_grad, unit_one, inverse_one, norm_gains[0]
    )
    input_grad = resid_grad + input_from_norm
    qkv_g, out_g, up_g, down_g = (
        lax.psum_scatter(
            qkv_part.astype(jnp.bfloat16), "dp", scatter_dimension=0, tiled=True
        ).astype(jnp.float32),
        lax.psum_scatter(
            out_weight_part.astype(jnp.bfloat16), "dp", scatter_dimension=0, tiled=True
        ).astype(jnp.float32),
        lax.psum_scatter(
            up_grad.astype(jnp.bfloat16), "dp", scatter_dimension=0, tiled=True
        ).astype(jnp.float32),
        lax.psum_scatter(
            down_grad.astype(jnp.bfloat16), "dp", scatter_dimension=0, tiled=True
        ).astype(jnp.float32),
    )
    width = biases.shape[1]
    gains_part = jnp.stack([gain_one_part, gain_two_part])
    biases_part = jnp.stack(
        [
            shift_one_part,
            shift_two_part,
            place(jnp.sum(query_low, axis=0, dtype=jnp.float32), width, rank),
            place(jnp.sum(value_low, axis=0, dtype=jnp.float32), width, rank),
            out_bias_part,
            down_bias_part,
        ]
    )
    qkv_m, qkv_s, qkv_dir = adam_terms(qkv_moment, qkv_square, qkv_g)
    out_m, out_s, out_dir = adam_terms(out_moment, out_square, out_g)
    up_m, up_s, up_dir = adam_terms(up_moment, up_square, up_g)
    down_m, down_s, down_dir = adam_terms(down_moment, down_square, down_g)
    local_sums = jnp.stack(
        [
            jnp.sum(qkv_weight * qkv_weight),
            jnp.sum(qkv_dir * qkv_dir),
            jnp.sum(out_weight * out_weight),
            jnp.sum(out_dir * out_dir),
            jnp.sum(up_weight * up_weight),
            jnp.sum(up_dir * up_dir),
            jnp.sum(down_weight * down_weight),
            jnp.sum(down_dir * down_dir),
        ]
    )
    gains_g, biases_g, upb_g = lax.psum((gains_part, biases_part, up_bias_part), ("dp", "tensor"))
    totals = lax.psum(local_sums, ("dp", "tensor"))
    norms = jnp.sqrt(totals).reshape(4, 2)
    qkv_n = qkv_weight - learn_rate * (norms[0, 0] / norms[0, 1]) * qkv_dir
    out_n = out_weight - learn_rate * (norms[1, 0] / norms[1, 1]) * out_dir
    up_n = up_weight - learn_rate * (norms[2, 0] / norms[2, 1]) * up_dir
    down_n = down_weight - learn_rate * (norms[3, 0] / norms[3, 1]) * down_dir
    gains_n, gains_m, gains_s = lamb_rows(norm_gains, gains_moment, gains_square, gains_g)
    biases_n, biases_m, biases_s = lamb_rows(biases, biases_moment, biases_square, biases_g)
    upb_n, upb_m, upb_s = lamb_rows(up_bias, up_bias_moment, up_bias_square, upb_g)
    return (
        output,
        input_grad,
        qkv_g,
        out_g,
        up_g,
        down_g,
        gains_g,
        biases_g,
        upb_g,
        qkv_n,
        out_n,
        up_n,
        down_n,
        gains_n,
        biases_n,
        upb_n,
        qkv_n.astype(jnp.bfloat16),
        out_n.astype(jnp.bfloat16),
        up_n.astype(jnp.bfloat16),
        down_n.astype(jnp.bfloat16),
        qkv_m,
        out_m,
        up_m,
        down_m,
        gains_m,
        biases_m,
        upb_m,
        qkv_s,
        out_s,
        up_s,
        down_s,
        gains_s,
        biases_s,
        upb_s,
        norms[:, 0],
        norms[:, 1],
    )


def solution(mesh):
    return jax.shard_map(
        per_device,
        mesh=mesh,
        in_specs=(
            P(("dp", "tensor"), None),
            P(("dp", "tensor"), None),
            P("dp"),
            P("dp", None, "tensor"),
            P("dp", None, "tensor"),
            P("dp", None, "tensor"),
            P("dp", "tensor"),
            P("dp", "tensor"),
            P("dp", "tensor"),
            P("dp", "tensor"),
            P("dp", "tensor"),
            P("dp", "tensor"),
            P("dp", "tensor"),
            P("dp", "tensor"),
            P("dp", "tensor"),
            P(),
            P(),
            P(),
            P(),
            P(),
            P(),
            P(),
            P(),
            P(),
        ),
        out_specs=(
            P(("dp", "tensor"), None),
            P(("dp", "tensor"), None),
            P("dp", None, "tensor"),
            P("dp", "tensor"),
            P("dp", "tensor"),
            P("dp", "tensor"),
            P(),
            P(),
            P(),
            P("dp", None, "tensor"),
            P("dp", "tensor"),
            P("dp", "tensor"),
            P("dp", "tensor"),
            P(),
            P(),
            P(),
            P("dp", None, "tensor"),
            P("dp", "tensor"),
            P("dp", "tensor"),
            P("dp", "tensor"),
            P("dp", None, "tensor"),
            P("dp", "tensor"),
            P("dp", "tensor"),
            P("dp", "tensor"),
            P(),
            P(),
            P(),
            P("dp", None, "tensor"),
            P("dp", "tensor"),
            P("dp", "tensor"),
            P("dp", "tensor"),
            P(),
            P(),
            P(),
            P(),
            P(),
        ),
        check_vma=False,
    )
```

profile of v0, /device:TPU:0, one launch (start us, length us, event | category | flops | bytes accessed | tf_op | source)
XLA Modules:
  0.0 828.6 jit_solution(16726841083446359867)
XLA Ops:
  7.3 1.8 copy.67
  13.5 2.1 fusion.54
  16.0 1.6 multiply_reduce_fusion.12
  17.6 34.4 %all_gather.30 = bf16[1024,256]{1,0:T(8,128)(2,1)S(1)} all-gather(bf16[128,256]{1,0:T(8,128)(2,1)S(1)} %get-tuple-element.302), channel_id=1, replica_groups=mesh['dp'=8,'tensor'=4] {'dp'}, dimensions={0}, use_global_device_ids=true | all-gather | bytes 589824 | tf_op jit(solution)/shard_map/all_gather | solution.py:120
  52.0 10.1 %all-gather.10.cloned.1.call-done = bf16[1024,3,256]{0,2,1:T(8,128)(2,1)} async-done(((bf16[128,3,256]{0,2,1:T(8,128)(2,1)}), bf16[1024,3,256]{0,2,1:T(8,128)(2,1)}) %all-gather.10.cloned.1.call-update) | async-done | bytes 1572880 | tf_op jit(solution)/shard_map/all_gather | solution.py:119
  62.1 22.6 %all-gather.8.cloned.1.call-done = bf16[1024,1024]{1,0:T(8,128)(2,1)} async-done(((bf16[256,1024]{1,0:T(8,128)(2,1)}), bf16[1024,1024]{1,0:T(8,128)(2,1)}) %all-gather.8.cloned.1.call-update) | async-done | bytes 2097168 | tf_op jit(solution)/shard_map/all_gather | solution.py:126
  84.8 3.9 fusion.40
  89.2 23.8 %while.27 = (s32[]{:T(128)}, bf16[2,512,256]{2,1,0:T(8,128)(2,1)S(1)}, f32[2,4,512]{2,1,0:T(4,128)S(1)}, s32[2]{0:T(128)S(1)}, s32[]{:T(128)}, /*index=5*/bf16[1...) while((s32[]{:T(128)}, ...), condition=%wide.region_5.6_spmd, body=%wide.region_2.5_spmd.sunk | while | flops 576716288 | bytes 38347504 | solution.py:146
  91.8 2.8 fusion.136
  94.6 3.0 fusion.137
  97.5 3.4 fusion.138
  103.7 2.8 fusion.136
  106.5 3.0 fusion.137
  109.4 3.4 fusion.138
  113.8 3.8 fusion.86
  119.2 43.2 %reduce-scatter.9.cloned.1.call-done = f32[256,1024]{1,0:T(8,128)} async-done(((f32[1024,1024]{1,0:T(8,128)}), f32[256,1024]{1,0:T(8,128)}) %reduce-scatter.9.cloned.1.call-update) | async-done | bytes 1048592 | tf_op jit(solution)/shard_map/reduce_scatter | solution.py:149
  162.4 1.4 fusion.81
  168.1 45.9 %all-gather.14.cloned.1.call-done = bf16[1024,1024]{1,0:T(8,128)(2,1)} async-done(((bf16[128,1024]{1,0:T(8,128)(2,1)}), bf16[1024,1024]{1,0:T(8,128)(2,1)}) %all-gather.14.cloned.1.call-update) | async-done | bytes 2097168 | tf_op jit(solution)/shard_map/all_gather | solution.py:121
  214.1 23.1 %all-gather.12.cloned.1.call-done = bf16[1024,1024]{1,0:T(8,128)(2,1)} async-done(((bf16[256,1024]{1,0:T(8,128)(2,1)}), bf16[1024,1024]{1,0:T(8,128)(2,1)}) %all-gather.12.cloned.1.call-update) | async-done | bytes 2097168 | tf_op jit(solution)/shard_map/all_gather | solution.py:158
  237.2 6.5 fusion.87
  243.7 17.5 %all-gather.18.cloned.1.call-done = bf16[1024,1024]{1,0:T(8,128)(2,1)} async-done(((bf16[256,1024]{1,0:T(8,128)(2,1)}), bf16[1024,1024]{1,0:T(8,128)(2,1)}) %all-gather.18.cloned.1.call-update) | async-done | bytes 2097168 | tf_op jit(solution)/shard_map/all_gather | solution.py:180
  261.2 51.8 %all-gather.16.cloned.1.call-done = bf16[1024,1024]{1,0:T(8,128)(2,1)} async-done(((bf16[128,1024]{1,0:T(8,128)(2,1)}), bf16[1024,1024]{1,0:T(8,128)(2,1)}) %all-gather.16.cloned.1.call-update) | async-done | bytes 2097168 | tf_op jit(solution)/shard_map/all_gather | solution.py:122
  313.0 8.7 %convert_reduce_fusion = (f32[1024]{0:T(1024)}, bf16[1024,1024]{1,0:T(8,128)(2,1)S(1)}) fusion(f32[1024,1024]{1,0:T(8,128)} %fusion.87, f32[1024]{0:T(1024)S(1)} %dynamic_slice.34, bf16[1024,1024]{1,0:T(8,128)(2,1)} %all-gather.18.cloned.1.call-done, bf16[1024,1024]{1,0:T(8,128)(2,1)} %all-gather.16.cloned.1.call-done), kind=kOutput, calls=%fused_computation.55 | convolution fusion | flops 2170551296 | bytes 10493952 | tf_op jit(solution)/shard_map/dot_general | solution.py:184
  323.0 4.3 fusion.88
  327.5 7.0 convolution_convert_fusion.1
  334.6 36.1 %reduce-scatter.13.cloned.1.call-done = f32[256,1024]{1,0:T(8,128)} async-done(((f32[1024,1024]{1,0:T(8,128)}), f32[256,1024]{1,0:T(8,128)}) %reduce-scatter.13.cloned.1.call-update) | async-done | bytes 1048592 | tf_op jit(solution)/shard_map/reduce_scatter | solution.py:189
  370.7 2.3 multiply_reduce_fusion.1
  373.0 31.4 %reduce-scatter.11.cloned.1.call-done = bf16[256,1024]{1,0:T(8,128)(2,1)} async-done(((bf16[1024,1024]{1,0:T(8,128)(2,1)}), bf16[256,1024]{1,0:T(8,128)(2,1)}) %reduce-scatter.11.cloned.1.call-update) | async-done | bytes 524304 | tf_op jit(solution)/shard_map/reduce_scatter | solution.py:163
  404.4 3.9 convert_reduce_fusion.4
  408.3 5.9 convolution_convert_fusion
  414.4 7.4 convert_bitcast_fusion
  421.8 9.2 %all-gather.20.cloned.1.call-done = bf16[1024,1024]{1,0:T(8,128)(2,1)} async-done(((bf16[256,1024]{1,0:T(8,128)(2,1)}), bf16[1024,1024]{1,0:T(8,128)(2,1)}) %all-gather.20.cloned.1.call-update) | async-done | bytes 2097168 | tf_op jit(solution)/shard_map/all_gather | solution.py:201
  431.0 3.2 convolution_convert_fusion.2
  434.5 3.2 convolution_convert_fusion.3
  437.8 32.4 %while.28 = (s32[]{:T(128)}, f32[1024,4,64]{0,2,1:T(8,128)S(1)}, f32[1024,4,64]{0,2,1:T(8,128)S(1)}, bf16[2,512,256]{1,2,0:T(8,128)(2,1)}, s32[2]{0:T(128)S(1)},...) while((s32[]{:T(128)}, f32[1024,4,64]{0,2,1:T(8,128)S(1)}, ...), condition=%wide.region_15.16_spmd.clone, body=%wide.region_13.15_spmd.clone.sunk | while | flops 1368915456 | bytes 82101112 | solution.py:237
  442.3 2.4 fusion.148
  444.7 3.9 multiply_reduce_fusion.20
  458.4 2.4 fusion.148
  460.9 3.9 multiply_reduce_fusion.20
  472.0 4.6 fusion.43
  477.0 4.6 bitcast_convert_fusion
  485.1 17.9 %reduce-scatter.21.cloned.1.call-done = bf16[128,1024]{1,0:T(8,128)(2,1)} async-done(((bf16[1024,1024]{1,0:T(8,128)(2,1)}), bf16[128,1024]{1,0:T(8,128)(2,1)}) %reduce-scatter.21.cloned.1.call-update) | async-done | bytes 262160 | tf_op jit(solution)/shard_map/reduce_scatter | solution.py:267
  503.0 3.0 multiply_reduce_fusion.7
  506.1 67.9 %reduce-scatter.23.cloned.1.call-done = bf16[128,1024]{1,0:T(8,128)(2,1)} async-done(((bf16[1024,1024]{1,0:T(8,128)(2,1)}), bf16[128,1024]{1,0:T(8,128)(2,1)}) %reduce-scatter.23.cloned.1.call-update) | async-done | bytes 262160 | tf_op jit(solution)/shard_map/reduce_scatter | solution.py:270
  573.9 2.8 multiply_reduce_fusion.5
  578.2 61.4 %reduce-scatter.19.cloned.1.call-done = bf16[128,256]{1,0:T(8,128)(2,1)} async-done(((bf16[1024,256]{1,0:T(8,128)(2,1)}), bf16[128,256]{1,0:T(8,128)(2,1)}) %reduce-scatter.19.cloned.1.call-update) | async-done | bytes 65552 | tf_op jit(solution)/shard_map/reduce_scatter | solution.py:264
  639.6 2.2 multiply_reduce_fusion.11
  641.8 66.3 %reduce-scatter.17.cloned.1.call-done = bf16[128,3,256]{2,0,1:T(8,128)(2,1)} async-done(((bf16[1024,3,256]{2,0,1:T(8,128)(2,1)}), bf16[128,3,256]{2,0,1:T(8,128)(2,1)}) %reduce-scatter.17.cloned.1.call-update) | async-done | bytes 196624 | tf_op jit(solution)/shard_map/reduce_scatter | solution.py:261
  708.1 2.9 multiply_reduce_fusion.9
  711.0 5.8 stack.85
  716.8 23.9 %reduce-scatter.15.cloned.1.call-done = bf16[256,1024]{1,0:T(8,128)(2,1)} async-done(((bf16[1024,1024]{1,0:T(8,128)(2,1)}), bf16[256,1024]{1,0:T(8,128)(2,1)}) %reduce-scatter.15.cloned.1.call-update) | async-done | bytes 524304 | tf_op jit(solution)/shard_map/reduce_scatter | solution.py:248
  740.7 2.2 fusion.60
  744.3 1.4 stack.76
  745.7 41.1 %all-reduce = (f32[2,1024]{1,0:T(2,128)}, f32[6,1024]{1,0:T(8,128)}, f32[4096]{0:T(1024)}, f32[8]{0:T(128)}) all-reduce(f32[2,1024]{1,0:T(2,128)} %pad_maximum_fusion.3, f32[6,1024]{1,0:T(8,128)} %stack.76, f32[4096]{0:T(1024)} %copy-done.30, f32[8]{0:T(128)} %stack.85), channel_id=1, replica_groups=mesh['dp'=8,'tensor'=4] {'dp','tensor'}, use_global_device_ids=true, to_apply=%region_25.26 | all-reduce | flops 12296 | bytes 98368 | tf_op jit(solution)/shard_map/psum | solution.py:302
  789.3 1.5 slice_reduce_fusion
  790.8 1.6 fusion.85
  800.2 2.0 multiply_reduce_fusion.15
  802.9 1.5 multiply_reduce_fusion.17
  809.4 1.4 multiply_subtract_fusion.4
  810.8 1.7 fusion.72
  812.5 2.0 fusion.73
  814.5 2.3 fusion.70
  816.8 2.3 fusion.71
  819.2 2.4 fusion.57
  (214 shorter events, 49.9 us)
Async XLA Ops:
  7.2 54.9 %all-gather.10.cloned.1.call-start = ((), (), s32[]{:S(2)}) async-start(), calls=%async_computation.9 | async-start | bytes 1769472 | tf_op jit(solution)/shard_map/all_gather | solution.py:119
  9.1 75.7 %all-gather.8.cloned.1.call-start = ((), (), s32[]{:S(2)}) async-start(), calls=%async_computation.8 | async-start | bytes 2621440 | tf_op jit(solution)/shard_map/all_gather | solution.py:126
  10.3 5.6 copy-start.31
  11.7 4.2 copy-start.34
  12.5 3.4 copy-start.28
  15.6 146.8 %reduce-scatter.9.cloned.1.call-start = ((), (), s32[]{:S(2)}) async-start(), calls=%async_computation.10 | async-start | bytes 5242880 | tf_op jit(solution)/shard_map/reduce_scatter | solution.py:149
  52.0 61.8 %copy-start.11 = (bf16[1024,256]{1,0:T(8,128)(2,1)}, bf16[1024,256]{1,0:T(8,128)(2,1)S(1)}, u32[]{:S(2)}) copy-start(bf16[1024,256]{1,0:T(8,128)(2,1)S(1)} %all_gather.30) | copy-start | bytes 1572868
  113.0 0.8 copy-start.16
  113.0 4.6 copy-start
  113.8 3.9 copy-start.9
  113.8 48.6 %copy-start.1 = (bf16[256,1024]{1,0:T(8,128)(2,1)S(1)}, bf16[256,1024]{1,0:T(8,128)(2,1)}, u32[]{:S(2)}) copy-start(bf16[256,1024]{1,0:T(8,128)(2,1)} %param.28) | copy-start | bytes 1572868
  117.7 48.2 %copy-start.7 = (f32[128,1024]{1,0:T(8,128)S(1)}, f32[128,1024]{1,0:T(8,128)}, u32[]{:S(2)}) copy-start(f32[128,1024]{1,0:T(8,128)} %param.40) | copy-start | bytes 1572868
  117.7 96.4 %all-gather.14.cloned.1.call-start = ((), (), s32[]{:S(2)}) async-start(), calls=%async_computation.12 | async-start | bytes 2359296 | tf_op jit(solution)/shard_map/all_gather | solution.py:121
  119.1 118.1 %all-gather.12.cloned.1.call-start = ((), (), s32[]{:S(2)}) async-start(), calls=%async_computation.11 | async-start | bytes 2621440 | tf_op jit(solution)/shard_map/all_gather | solution.py:158
  165.2 96.0 %all-gather.18.cloned.1.call-start = ((), (), s32[]{:S(2)}) async-start(), calls=%async_computation.15 | async-start | bytes 2621440 | tf_op jit(solution)/shard_map/all_gather | solution.py:180
  165.8 147.2 %all-gather.16.cloned.1.call-start = ((), (), s32[]{:S(2)}) async-start(), calls=%async_computation.13 | async-start | bytes 2359296 | tf_op jit(solution)/shard_map/all_gather | solution.py:122
  167.2 203.5 %reduce-scatter.13.cloned.1.call-start = ((), (), s32[]{:S(2)}) async-start(), calls=%async_computation.16 | async-start | bytes 5242880 | tf_op jit(solution)/shard_map/reduce_scatter | solution.py:189
  313.0 10.0 %copy-start.39 = (bf16[1024,1024]{1,0:T(8,128)(2,1)S(1)}, bf16[1024,1024]{1,0:T(8,128)(2,1)}, u32[]{:S(2)}) copy-start(bf16[1024,1024]{1,0:T(8,128)(2,1)} %all-gather.14.cloned.1.call-done) | copy-start | bytes 6291460
  321.7 1.3 copy-start.40
  327.4 77.0 %reduce-scatter.11.cloned.1.call-start = ((), (), s32[]{:S(2)}) async-start(), calls=%async_computation.14 | async-start | bytes 2621440 | tf_op jit(solution)/shard_map/reduce_scatter | solution.py:163
  334.5 69.9 %copy-start.6 = (bf16[256,1024]{1,0:T(8,128)(2,1)S(1)}, bf16[256,1024]{1,0:T(8,128)(2,1)}, u32[]{:S(2)}) copy-start(bf16[256,1024]{1,0:T(8,128)(2,1)} %param.29) | copy-start | bytes 1572868
  334.5 96.5 %all-gather.20.cloned.1.call-start = ((), (), s32[]{:S(2)}) async-start(), calls=%async_computation.17 | async-start | bytes 2621440 | tf_op jit(solution)/shard_map/all_gather | solution.py:201
  408.3 94.8 %reduce-scatter.21.cloned.1.call-start = ((), (), s32[]{:S(2)}) async-start(), calls=%async_computation.21 | async-start | bytes 2359296 | tf_op jit(solution)/shard_map/reduce_scatter | solution.py:267
  414.3 159.6 %reduce-scatter.23.cloned.1.call-start = ((), (), s32[]{:S(2)}) async-start(), calls=%async_computation.22 | async-start | bytes 2359296 | tf_op jit(solution)/shard_map/reduce_scatter | solution.py:270
  421.8 217.8 %reduce-scatter.19.cloned.1.call-start = ((), (), s32[]{:S(2)}) async-start(), calls=%async_computation.20 | async-start | bytes 589824 | tf_op jit(solution)/shard_map/reduce_scatter | solution.py:264
  434.3 273.8 %reduce-scatter.17.cloned.1.call-start = ((), (), s32[]{:S(2)}) async-start(), calls=%async_computation.19 | async-start | bytes 1769472 | tf_op jit(solution)/shard_map/reduce_scatter | solution.py:261
  448.6 1.1 copy-start.3
  452.1 1.1 copy-start.12
  453.2 0.8 copy-start.13
  464.8 1.0 copy-start.3
  468.3 1.1 copy-start.12
  469.3 0.8 copy-start.13
  476.7 5.0 copy-start.26
  476.7 6.3 copy-start.27
  476.7 6.9 copy-start.21
  476.7 7.5 copy-start.5
  476.7 8.2 copy-start.38
  476.7 26.3 %copy-start.18 = (f32[128,1024]{1,0:T(8,128)S(1)}, f32[128,1024]{1,0:T(8,128)}, u32[]{:S(2)}) copy-start(f32[128,1024]{1,0:T(8,128)} %param.39) | copy-start | bytes 1572868
  476.7 263.9 %reduce-scatter.15.cloned.1.call-start = ((), (), s32[]{:S(2)}) async-start(), calls=%async_computation.18 | async-start | bytes 2621440 | tf_op jit(solution)/shard_map/reduce_scatter | solution.py:248
  481.6 92.3 %copy-start.19 = (f32[128,1024]{1,0:T(8,128)S(1)}, f32[128,1024]{1,0:T(8,128)}, u32[]{:S(2)}) copy-start(f32[128,1024]{1,0:T(8,128)} %param.42) | copy-start | bytes 1572868
  481.6 92.3 %copy-start.20 = (f32[128,1024]{1,0:T(8,128)S(1)}, f32[128,1024]{1,0:T(8,128)}, u32[]{:S(2)}) copy-start(f32[128,1024]{1,0:T(8,128)} %param.41) | copy-start | bytes 1572868
  481.6 95.3 %copy-start.14 = (bf16[2,512,256]{1,2,0:T(8,128)(2,1)S(1)}, bf16[2,512,256]{1,2,0:T(8,128)(2,1)}, u32[]{:S(2)}) copy-start(bf16[2,512,256]{1,2,0:T(8,128)(2,1)} %get-tuple-element.150) | copy-start | bytes 1572868
  481.6 158.0 %copy-start.22 = (f32[128,256]{1,0:T(8,128)S(1)}, f32[128,256]{1,0:T(8,128)}, u32[]{:S(2)}) copy-start(f32[128,256]{1,0:T(8,128)} %param.36) | copy-start | bytes 393220
  481.6 158.0 %copy-start.23 = (f32[128,256]{1,0:T(8,128)S(1)}, f32[128,256]{1,0:T(8,128)}, u32[]{:S(2)}) copy-start(f32[128,256]{1,0:T(8,128)} %param.35) | copy-start | bytes 393220
  485.1 156.7 %copy-start.30 = (f32[4096]{0:T(1024)}, f32[4096]{0:T(1024)S(1)}, u32[]{:S(2)}) copy-start(f32[4096]{0:T(1024)S(1)} %dynamic_update_slice.24) | copy-start | bytes 49156
  485.1 255.5 %copy-start.2 = (bf16[256,1024]{1,0:T(8,128)(2,1)S(1)}, bf16[256,1024]{1,0:T(8,128)(2,1)}, u32[]{:S(2)}) copy-start(bf16[256,1024]{1,0:T(8,128)(2,1)} %param.28) | copy-start | bytes 1572868
  576.8 237.7 %copy-start.8 = (f32[128,1024]{1,0:T(8,128)S(1)}, f32[128,1024]{1,0:T(8,128)}, u32[]{:S(2)}) copy-start(f32[128,1024]{1,0:T(8,128)} %param.40) | copy-start | bytes 1572868
  578.2 63.6 %copy-start.33 = (f32[1,1024]{1,0:T(1,128)}, f32[1,1024]{1,0:T(1,128)S(1)}, u32[]{:S(2)}) copy-start(f32[1,1024]{1,0:T(1,128)S(1)} %constant_dynamic-update-slice_fusion.1) | copy-start | bytes 12292
  641.8 175.0 %copy-start.17 = (f32[128,256]{1,0:T(8,128)}, f32[128,256]{1,0:T(8,128)S(1)}, u32[]{:S(2)}) copy-start(f32[128,256]{1,0:T(8,128)S(1)} %get-tuple-element.275) | copy-start | bytes 393220
  641.8 175.0 %copy-start.10 = (f32[128,1024]{1,0:T(8,128)S(1)}, f32[128,1024]{1,0:T(8,128)}, u32[]{:S(2)}) copy-start(f32[128,1024]{1,0:T(8,128)} %param.37) | copy-start | bytes 1572868
  711.0 108.1 %copy-start.15 = (f32[128,3,256]{2,0,1:T(8,128)}, f32[128,3,256]{2,0,1:T(8,128)S(1)}, u32[]{:S(2)}) copy-start(f32[128,3,256]{2,0,1:T(8,128)S(1)} %get-tuple-element.279) | copy-start | bytes 1179652
  742.9 76.2 %copy-start.4 = (f32[256,1024]{1,0:T(8,128)S(1)}, f32[256,1024]{1,0:T(8,128)}, u32[]{:S(2)}) copy-start(f32[256,1024]{1,0:T(8,128)} %get-tuple-element.284) | copy-start | bytes 3145732
  806.4 12.8 %copy-start.29 = (f32[1,1024]{1,0:T(1,128)S(1)}, f32[1,1024]{1,0:T(1,128)}, u32[]{:S(2)}) copy-start(f32[1,1024]{1,0:T(1,128)} %copy-done.28) | copy-start | bytes 12292
  806.4 12.8 %copy-start.32 = (f32[256]{0:T(256)S(1)}, f32[256]{0:T(256)}, u32[]{:S(2)}) copy-start(f32[256]{0:T(256)} %copy-done.31) | copy-start | bytes 3076
  806.4 12.8 %copy-start.35 = (f32[256]{0:T(256)S(1)}, f32[256]{0:T(256)}, u32[]{:S(2)}) copy-start(f32[256]{0:T(256)} %copy-done.34) | copy-start | bytes 3076
  806.4 12.8 %copy-start.36 = (f32[256]{0:T(256)S(1)}, f32[256]{0:T(256)}, u32[]{:S(2)}) copy-start(f32[256]{0:T(256)} %broadcast_multiply_fusion) | copy-start | bytes 3076
  806.4 12.8 %copy-start.37 = (f32[256]{0:T(256)S(1)}, f32[256]{0:T(256)}, u32[]{:S(2)}) copy-start(f32[256]{0:T(256)} %broadcast_multiply_fusion.1) | copy-start | bytes 3076
  807.3 14.3 %copy-start.24 = (f32[6,1024]{1,0:T(8,128)}, f32[6,1024]{1,0:T(8,128)S(1)}, u32[]{:S(2)}) copy-start(f32[6,1024]{1,0:T(8,128)S(1)} %get-tuple-element.260) | copy-start | bytes 73732
  807.3 14.3 %copy-start.25 = (f32[6,1024]{1,0:T(8,128)}, f32[6,1024]{1,0:T(8,128)S(1)}, u32[]{:S(2)}) copy-start(f32[6,1024]{1,0:T(8,128)S(1)} %get-tuple-element.261) | copy-start | bytes 73732
Sparse Core Ops, SparseCore 0:
  10.6 51.4 all-gather.9
  64.3 20.4 all-gather.7
  117.8 44.5 reduce-scatter.8
  165.0 49.0 all-gather.13
  216.1 21.0 all-gather.11
  238.6 22.5 all-gather.17
  263.9 49.0 all-gather.15
  327.5 43.1 reduce-scatter.12
  373.2 31.1 reduce-scatter.10
  408.4 22.5 all-gather.19
  434.6 68.4 reduce-scatter.20
  506.4 67.4 reduce-scatter.22
  577.8 61.7 reduce-scatter.18
  642.9 65.1 reduce-scatter.16
  710.5 30.1 reduce-scatter.14
where the time goes:
time: 839 us; the launch traced here: 829 us
  waiting for transfers between devices  529 us (63%)
  matrix products  94.9 us (11%)
  blocking collectives  75.5 us (9%)
  other arithmetic  71.6 us (9%)
  local copies, waits for them, and re-layouts  27.6 us (3%)
  between operations  21.6 us (3%)
    reduce_scatter x1, waiting for transfers between devices, per_device(): lax.psum_scatter(down_grad.astype(jnp.bfloat16), 'dp', scatter_dimension=...  67.9 us
    reduce_scatter x1, waiting for transfers between devices, per_device(): lax.psum_scatter(qkv_part.astype(jnp.bfloat16), 'dp', scatter_dimension=0...  66.3 us
    reduce_scatter x1, waiting for transfers between devices, per_device(): lax.psum_scatter(out_weight_part.astype(jnp.bfloat16), 'dp', scatter_dime...  61.4 us
    all_gather x1, waiting for transfers between devices, per_device(): lax.all_gather(shards[3], 'dp', axis=0, tiled=True)  51.8 us
    all_gather x1, waiting for transfers between devices, per_device(): lax.all_gather(shards[2], 'dp', axis=0, tiled=True)  45.9 us
    reduce_scatter x1, waiting for transfers between devices, per_device(): lax.psum_scatter(jnp.einsum('le,de->ld', piece, out_full, preferred_eleme...  43.2 us
    psum x1, blocking collectives, per_device(): lax.psum((gains_part, biases_part, up_bias_part), ('dp', 'tensor'))  41.1 us
    reduce_scatter x1, waiting for transfers between devices, per_device(): lax.psum_scatter(jnp.einsum('lf,df->ld', piece, up_full, preferred_elemen...  36.1 us
  transfers between devices with their start and end apart: 15, of which 15 were waited for; matrix products, arithmetic and copies ran while one was open for 13% of the time, Pallas kernels for 0%

commit v1 on v0

--- a/solution.py
+++ b/solution.py
@@ -2,6 +2,7 @@
 import jax.numpy as jnp
 from jax import lax
 from jax.sharding import PartitionSpec as P
+from jax.lax import axis_index, axis_size, ppermute
 
 HEADS = 16
 HEAD = 64
@@ -155,7 +156,21 @@
     resid = x_rows + (attn_rows + biases[4])
     normed_two, unit_two, inverse_two = norm_forward(resid, norm_gains[1], biases[1])
     normed_two_low = normed_two.astype(jnp.bfloat16)
-    normed_two_all = lax.all_gather(normed_two_low, "tensor", axis=0, tiled=True)
+    high = axis_size("tensor")
+    p_next, parts_out, response = (high, axis_index("tensor"), normed_two_low.shape[0])
+    normed_two_all = jnp.zeros(
+        (*normed_two_low.shape[:0], p_next * response, *normed_two_low.shape[1:]),
+        normed_two_low.dtype,
+    )
+    new = normed_two_low
+    row_list = tuple(((to_i, (to_i + 1) % p_next) for to_i in range(p_next)))
+    for ix in range(p_next):
+        oldest = (parts_out - ix) % p_next
+        normed_two_all = lax.dynamic_update_slice_in_dim(
+            normed_two_all, new, oldest * response, axis=0
+        )
+        if ix < p_next - 1:
+            new = ppermute(new, "tensor", row_list)
     up_slice = lax.dynamic_slice_in_dim(up_bias, rank * local_hidden, local_hidden)
     pre = jnp.dot(normed_two_all, up_full, preferred_element_type=jnp.float32) + up_slice
     hidden_low = gelu_value(pre).astype(jnp.bfloat16)

time: 839 us -> 814 us (0.970)
  waiting for transfers between devices: 529 us -> 500 us
    all_gather x1, waiting for transfers between devices: 45.9 us -> 19.4 us  [per_device(): lax.all_gather(shards[2], 'dp', axis=0, tiled=True)]
    ppermute x0 -> x3, waiting for transfers between devices: none -> 23.5 us  [per_device(): new = ppermute(new, 'tensor', row_list)]
    all_gather x1 -> x0, waiting for transfers between devices: 23.1 us -> none  [per_device(): lax.all_gather(normed_two_low, 'tensor', axis=0, tiled=True)]
  transfers between devices with their start and end apart: 15 -> 17, of which waited for: 15 -> 17; matrix products, arithmetic and copies ran while one was open for 13% -> 14% of each run, Pallas kernels for 0% -> 0%
where the time goes in v1:
time: 814 us; the launch traced here: 804 us
  waiting for transfers between devices  500 us (61%)
  matrix products  94.3 us (12%)
  blocking collectives  75.6 us (9%)
  other arithmetic  71.6 us (9%)
  local copies, waits for them, and re-layouts  32.8 us (4%)
  between operations  21.7 us (3%)
    reduce_scatter x1, waiting for transfers between devices, per_device(): lax.psum_scatter(down_grad.astype(jnp.bfloat16), 'dp', scatter_dimension=...  68 us
    reduce_scatter x1, waiting for transfers between devices, per_device(): lax.psum_scatter(qkv_part.astype(jnp.bfloat16), 'dp', scatter_dimension=0...  66.6 us
    reduce_scatter x1, waiting for transfers between devices, per_device(): lax.psum_scatter(out_weight_part.astype(jnp.bfloat16), 'dp', scatter_dime...  61.3 us
    all_gather x1, waiting for transfers between devices, per_device(): lax.all_gather(shards[3], 'dp', axis=0, tiled=True)  51.7 us
    reduce_scatter x1, waiting for transfers between devices, per_device(): lax.psum_scatter(jnp.einsum('le,de->ld', piece, out_full, preferred_eleme...  41.2 us
    psum x1, blocking collectives, per_device(): lax.psum((gains_part, biases_part, up_bias_part), ('dp', 'tensor'))  41.1 us
    reduce_scatter x1, waiting for transfers between devices, per_device(): lax.psum_scatter(jnp.einsum('lf,df->ld', piece, up_full, preferred_elemen...  36.1 us
    all_gather x1, blocking collectives, per_device(): lax.all_gather(shards[1], 'dp', axis=0, tiled=True)  34.5 us
  transfers between devices with their start and end apart: 17, of which 17 were waited for; matrix products, arithmetic and copies ran while one was open for 14% of the time, Pallas kernels for 0%

profile of v1, /device:TPU:0, one launch (start us, length us, event | category | flops | bytes accessed | tf_op | source)
XLA Modules:
  0.0 803.7 jit_solution(2713885596839587949)
XLA Ops:
  7.3 1.8 copy.67
  13.5 2.1 fusion.54
  16.0 1.6 multiply_reduce_fusion.12
  17.6 34.5 %all_gather.27 = bf16[1024,256]{1,0:T(8,128)(2,1)S(1)} all-gather(bf16[128,256]{1,0:T(8,128)(2,1)S(1)} %get-tuple-element.304), channel_id=1, replica_groups=mesh['dp'=8,'tensor'=4] {'dp'}, dimensions={0}, use_global_device_ids=true | all-gather | bytes 589824 | tf_op jit(solution)/shard_map/all_gather | solution.py:121
  52.1 10.1 %all-gather.9.cloned.1.call-done = bf16[1024,3,256]{0,2,1:T(8,128)(2,1)} async-done(((bf16[128,3,256]{0,2,1:T(8,128)(2,1)}), bf16[1024,3,256]{0,2,1:T(8,128)(2,1)}) %all-gather.9.cloned.1.call-update) | async-done | bytes 1572880 | tf_op jit(solution)/shard_map/all_gather | solution.py:120
  62.2 22.6 %all-gather.7.cloned.1.call-done = bf16[1024,1024]{1,0:T(8,128)(2,1)} async-done(((bf16[256,1024]{1,0:T(8,128)(2,1)}), bf16[1024,1024]{1,0:T(8,128)(2,1)}) %all-gather.7.cloned.1.call-update) | async-done | bytes 2097168 | tf_op jit(solution)/shard_map/all_gather | solution.py:127
  84.7 3.9 fusion.40
  89.2 23.8 %while.27 = (s32[]{:T(128)}, bf16[2,512,256]{2,1,0:T(8,128)(2,1)S(1)}, f32[2,4,512]{2,1,0:T(4,128)S(1)}, s32[2]{0:T(128)S(1)}, s32[]{:T(128)}, /*index=5*/bf16[1...) while((s32[]{:T(128)}, ...), condition=%wide.region_5.6_spmd, body=%wide.region_2.5_spmd.sunk | while | flops 576716288 | bytes 38347504 | solution.py:147
  91.7 2.8 fusion.138
  94.5 3.0 fusion.139
  97.5 3.4 fusion.140
  103.6 2.8 fusion.138
  106.4 3.0 fusion.139
  109.4 3.4 fusion.140
  113.8 3.8 fusion.88
  121.2 41.2 %reduce-scatter.9.cloned.1.call-done = f32[256,1024]{1,0:T(8,128)} async-done(((f32[1024,1024]{1,0:T(8,128)}), f32[256,1024]{1,0:T(8,128)}) %reduce-scatter.9.cloned.1.call-update) | async-done | bytes 1048592 | tf_op jit(solution)/shard_map/reduce_scatter | solution.py:150
  164.0 1.6 broadcast_in_dim.48
  166.6 8.6 %collective-permute-done = bf16[256,1024]{1,0:T(8,128)(2,1)S(1)} collective-permute-done((bf16[256,1024]{1,0:T(8,128)(2,1)S(1)}, bf16[256,1024]{1,0:T(8,128)(2,1)S(1)}, u32[]{:S(2)}, u32[]{:S(2)}) %collective-permute-start) | collective-permute-done | bytes 524320 | tf_op jit(solution)/shard_map/ppermute | solution.py:173
  175.2 8.6 %collective-permute-done.1 = bf16[256,1024]{1,0:T(8,128)(2,1)S(1)} collective-permute-done((bf16[256,1024]{1,0:T(8,128)(2,1)S(1)}, bf16[256,1024]{1,0:T(8,128)(2,1)S(1)}, u32[]{:S(2)}, u32[]{:S(2)}) %collective-permute-start.1) | collective-permute-done | bytes 524320 | tf_op jit(solution)/shard_map/ppermute | solution.py:173
  186.4 6.3 collective-permute-done.2
  192.7 1.9 constant_dynamic-update-slice_fusion.3
  194.6 19.4 %all-gather.11.cloned.1.call-done = bf16[1024,1024]{1,0:T(8,128)(2,1)} async-done(((bf16[128,1024]{1,0:T(8,128)(2,1)}), bf16[1024,1024]{1,0:T(8,128)(2,1)}) %all-gather.11.cloned.1.call-update) | async-done | bytes 2097168 | tf_op jit(solution)/shard_map/all_gather | solution.py:122
  214.0 6.5 fusion.89
  220.5 16.0 %all-gather.15.cloned.1.call-done = bf16[1024,1024]{1,0:T(8,128)(2,1)} async-done(((bf16[256,1024]{1,0:T(8,128)(2,1)}), bf16[1024,1024]{1,0:T(8,128)(2,1)}) %all-gather.15.cloned.1.call-update) | async-done | bytes 2097168 | tf_op jit(solution)/shard_map/all_gather | solution.py:195
  236.5 51.7 %all-gather.13.cloned.1.call-done = bf16[1024,1024]{1,0:T(8,128)(2,1)} async-done(((bf16[128,1024]{1,0:T(8,128)(2,1)}), bf16[1024,1024]{1,0:T(8,128)(2,1)}) %all-gather.13.cloned.1.call-update) | async-done | bytes 2097168 | tf_op jit(solution)/shard_map/all_gather | solution.py:123
  288.2 8.7 %convert_reduce_fusion = (f32[1024]{0:T(1024)}, bf16[1024,1024]{1,0:T(8,128)(2,1)S(1)}) fusion(f32[1024,1024]{1,0:T(8,128)} %fusion.89, f32[1024]{0:T(1024)S(1)} %dynamic_slice.34, bf16[1024,1024]{1,0:T(8,128)(2,1)} %all-gather.15.cloned.1.call-done, bf16[1024,1024]{1,0:T(8,128)(2,1)} %all-gather.13.cloned.1.call-done), kind=kOutput, calls=%fused_computation.55 | convolution fusion | flops 2170551296 | bytes 10493952 | tf_op jit(solution)/shard_map/dot_general | solution.py:199
  298.3 4.3 fusion.90
  302.7 7.0 convolution_convert_fusion.1
  309.8 36.1 %reduce-scatter.13.cloned.1.call-done = f32[256,1024]{1,0:T(8,128)} async-done(((f32[1024,1024]{1,0:T(8,128)}), f32[256,1024]{1,0:T(8,128)}) %reduce-scatter.13.cloned.1.call-update) | async-done | bytes 1048592 | tf_op jit(solution)/shard_map/reduce_scatter | solution.py:204
  345.9 2.3 multiply_reduce_fusion.1
  348.2 31.4 %reduce-scatter.11.cloned.1.call-done = bf16[256,1024]{1,0:T(8,128)(2,1)} async-done(((bf16[1024,1024]{1,0:T(8,128)(2,1)}), bf16[256,1024]{1,0:T(8,128)(2,1)}) %reduce-scatter.11.cloned.1.call-update) | async-done | bytes 524304 | tf_op jit(solution)/shard_map/reduce_scatter | solution.py:178
  379.6 3.9 convert_reduce_fusion.4
  383.8 6.1 convolution_convert_fusion
  389.9 6.6 convert_bitcast_fusion
  396.7 9.5 %all-gather.17.cloned.1.call-done = bf16[1024,1024]{1,0:T(8,128)(2,1)} async-done(((bf16[256,1024]{1,0:T(8,128)(2,1)}), bf16[1024,1024]{1,0:T(8,128)(2,1)}) %all-gather.17.cloned.1.call-update) | async-done | bytes 2097168 | tf_op jit(solution)/shard_map/all_gather | solution.py:216
  406.2 3.2 convolution_convert_fusion.2
  409.5 3.2 convolution_convert_fusion.3
  412.8 32.4 %while.28 = (s32[]{:T(128)}, f32[1024,4,64]{0,2,1:T(8,128)S(1)}, f32[1024,4,64]{0,2,1:T(8,128)S(1)}, bf16[2,512,256]{1,2,0:T(8,128)(2,1)}, s32[2]{0:T(128)S(1)},...) while((s32[]{:T(128)}, f32[1024,4,64]{0,2,1:T(8,128)S(1)}, ...), condition=%wide.region_15.16_spmd.clone, body=%wide.region_13.15_spmd.clone.sunk | while | flops 1368915456 | bytes 82101112 | solution.py:252
  417.2 2.4 fusion.150
  419.7 3.9 multiply_reduce_fusion.20
  433.5 2.4 fusion.150
  435.9 3.9 multiply_reduce_fusion.20
  447.1 4.6 fusion.43
  452.1 4.6 bitcast_convert_fusion
  460.2 17.8 %reduce-scatter.21.cloned.1.call-done = bf16[128,1024]{1,0:T(8,128)(2,1)} async-done(((bf16[1024,1024]{1,0:T(8,128)(2,1)}), bf16[128,1024]{1,0:T(8,128)(2,1)}) %reduce-scatter.21.cloned.1.call-update) | async-done | bytes 262160 | tf_op jit(solution)/shard_map/reduce_scatter | solution.py:282
  478.1 3.0 multiply_reduce_fusion.7
  481.1 68.0 %reduce-scatter.23.cloned.1.call-done = bf16[128,1024]{1,0:T(8,128)(2,1)} async-done(((bf16[1024,1024]{1,0:T(8,128)(2,1)}), bf16[128,1024]{1,0:T(8,128)(2,1)}) %reduce-scatter.23.cloned.1.call-update) | async-done | bytes 262160 | tf_op jit(solution)/shard_map/reduce_scatter | solution.py:285
  549.1 2.8 multiply_reduce_fusion.5
  553.3 61.3 %reduce-scatter.19.cloned.1.call-done = bf16[128,256]{1,0:T(8,128)(2,1)} async-done(((bf16[1024,256]{1,0:T(8,128)(2,1)}), bf16[128,256]{1,0:T(8,128)(2,1)}) %reduce-scatter.19.cloned.1.call-update) | async-done | bytes 65552 | tf_op jit(solution)/shard_map/reduce_scatter | solution.py:279
  614.6 2.2 multiply_reduce_fusion.11
  616.8 66.6 %reduce-scatter.17.cloned.1.call-done = bf16[128,3,256]{2,0,1:T(8,128)(2,1)} async-done(((bf16[1024,3,256]{2,0,1:T(8,128)(2,1)}), bf16[128,3,256]{2,0,1:T(8,128)(2,1)}) %reduce-scatter.17.cloned.1.call-update) | async-done | bytes 196624 | tf_op jit(solution)/shard_map/reduce_scatter | solution.py:276
  683.4 2.9 multiply_reduce_fusion.9
  686.3 5.8 stack.85
  692.1 23.7 %reduce-scatter.15.cloned.1.call-done = bf16[256,1024]{1,0:T(8,128)(2,1)} async-done(((bf16[1024,1024]{1,0:T(8,128)(2,1)}), bf16[256,1024]{1,0:T(8,128)(2,1)}) %reduce-scatter.15.cloned.1.call-update) | async-done | bytes 524304 | tf_op jit(solution)/shard_map/reduce_scatter | solution.py:263
  715.8 2.2 fusion.60
  720.8 41.1 %all-reduce = (f32[2,1024]{1,0:T(2,128)}, f32[6,1024]{1,0:T(8,128)}, f32[4096]{0:T(1024)}, f32[8]{0:T(128)}) all-reduce(f32[2,1024]{1,0:T(2,128)} %pad_maximum_fusion.3, f32[6,1024]{1,0:T(8,128)} %stack.76, f32[4096]{0:T(1024)} %copy-done.30, f32[8]{0:T(128)} %stack.85), channel_id=1, replica_groups=mesh['dp'=8,'tensor'=4] {'dp','tensor'}, use_global_device_ids=true, to_apply=%region_25.26 | all-reduce | flops 12296 | bytes 98368 | tf_op jit(solution)/shard_map/psum | solution.py:317
  764.4 1.5 slice_reduce_fusion
  765.9 1.6 fusion.87
  775.3 2.0 multiply_reduce_fusion.15
  786.0 1.7 fusion.74
  787.7 2.0 fusion.75
  789.7 2.3 fusion.72
  792.0 2.3 fusion.73
  794.3 2.4 fusion.57
  (223 shorter events, 57.4 us)
Async XLA Ops:
  7.2 55.0 %all-gather.9.cloned.1.call-start = ((), (), s32[]{:S(2)}) async-start(), calls=%async_computation.9 | async-start | bytes 1769472 | tf_op jit(solution)/shard_map/all_gather | solution.py:120
  9.1 75.6 %all-gather.7.cloned.1.call-start = ((), (), s32[]{:S(2)}) async-start(), calls=%async_computation.8 | async-start | bytes 2621440 | tf_op jit(solution)/shard_map/all_gather | solution.py:127
  10.3 5.6 copy-start.31
  11.7 76.9 %copy-start.34 = (f32[256]{0:T(256)}, f32[256]{0:T(256)S(1)}, u32[]{:S(2)}) copy-start(f32[256]{0:T(256)S(1)} %add_rsqrt_fusion.1) | copy-start | bytes 3076
  12.5 3.4 copy-start.28
  15.6 146.7 %reduce-scatter.9.cloned.1.call-start = ((), (), s32[]{:S(2)}) async-start(), calls=%async_computation.10 | async-start | bytes 5242880 | tf_op jit(solution)/shard_map/reduce_scatter | solution.py:150
  52.1 61.7 %copy-start.11 = (bf16[1024,256]{1,0:T(8,128)(2,1)}, bf16[1024,256]{1,0:T(8,128)(2,1)S(1)}, u32[]{:S(2)}) copy-start(bf16[1024,256]{1,0:T(8,128)(2,1)S(1)} %all_gather.27) | copy-start | bytes 1572868
  113.0 0.8 copy-start.16
  113.0 4.6 copy-start
  113.8 3.9 copy-start.9
  117.6 2.1 copy-start.7
  117.6 44.8 %copy-start.1 = (bf16[256,1024]{1,0:T(8,128)(2,1)S(1)}, bf16[256,1024]{1,0:T(8,128)(2,1)}, u32[]{:S(2)}) copy-start(bf16[256,1024]{1,0:T(8,128)(2,1)} %param.28) | copy-start | bytes 1572868
  117.6 96.4 %all-gather.11.cloned.1.call-start = ((), (), s32[]{:S(2)}) async-start(), calls=%async_computation.11 | async-start | bytes 2359296 | tf_op jit(solution)/shard_map/all_gather | solution.py:122
  119.0 117.5 %all-gather.15.cloned.1.call-start = ((), (), s32[]{:S(2)}) async-start(), calls=%async_computation.14 | async-start | bytes 2621440 | tf_op jit(solution)/shard_map/all_gather | solution.py:195
  119.6 168.6 %all-gather.13.cloned.1.call-start = ((), (), s32[]{:S(2)}) async-start(), calls=%async_computation.12 | async-start | bytes 2359296 | tf_op jit(solution)/shard_map/all_gather | solution.py:123
  121.1 224.8 %reduce-scatter.13.cloned.1.call-start = ((), (), s32[]{:S(2)}) async-start(), calls=%async_computation.15 | async-start | bytes 5242880 | tf_op jit(solution)/shard_map/reduce_scatter | solution.py:204
  166.6 8.6 %collective-permute-start = (bf16[256,1024]{1,0:T(8,128)(2,1)S(1)}, bf16[256,1024]{1,0:T(8,128)(2,1)S(1)}, u32[]{:S(2)}, u32[]{:S(2)}) collective-permute-start(bf16[256,1024]{1,0:T(8,128)(2,1)S(1)} %get-tuple-element.288), channel_id=1, source_target_pairs={{0,1},{1,2},{2,3},{3,0},{4,5},{5,6},{6,7},{7,4},{8,9},{9,10},{10,1... | collective-permute-start | bytes 1572872 | tf_op jit(solution)/shard_map/ppermute | solution.py:173
  175.2 8.6 %collective-permute-start.1 = (bf16[256,1024]{1,0:T(8,128)(2,1)S(1)}, bf16[256,1024]{1,0:T(8,128)(2,1)S(1)}, u32[]{:S(2)}, u32[]{:S(2)}) collective-permute-start(bf16[256,1024]{1,0:T(8,128)(2,1)S(1)} %collective-permute-done), channel_id=1, source_target_pairs={{0,1},{1,2},{2,3},{3,0},{4,5},{5,6},{6,7},{7,4},{8,9},{9,10},{10,1... | collective-permute-start | bytes 1572872 | tf_op jit(solution)/shard_map/ppermute | solution.py:173
  183.9 8.9 %collective-permute-start.2 = (bf16[256,1024]{1,0:T(8,128)(2,1)S(1)}, bf16[256,1024]{1,0:T(8,128)(2,1)}, u32[]{:S(2)}, u32[]{:S(2)}) collective-permute-start(bf16[256,1024]{1,0:T(8,128)(2,1)S(1)} %collective-permute-done.1), channel_id=1, source_target_pairs={{0,1},{1,2},{2,3},{3,0},{4,5},{5,6},{6,7},{7,4},{8,9},{9,10},{10,1... | collective-permute-start | bytes 1572872 | tf_op jit(solution)/shard_map/ppermute | solution.py:173
  288.2 10.0 %copy-start.40 = (bf16[1024,1024]{1,0:T(8,128)(2,1)S(1)}, bf16[1024,1024]{1,0:T(8,128)(2,1)}, u32[]{:S(2)}) copy-start(bf16[1024,1024]{1,0:T(8,128)(2,1)} %all-gather.11.cloned.1.call-done) | copy-start | bytes 6291460
  296.9 1.3 copy-start.41
  302.6 77.0 %reduce-scatter.11.cloned.1.call-start = ((), (), s32[]{:S(2)}) async-start(), calls=%async_computation.13 | async-start | bytes 2621440 | tf_op jit(solution)/shard_map/reduce_scatter | solution.py:178
  309.7 69.9 %copy-start.6 = (bf16[256,1024]{1,0:T(8,128)(2,1)S(1)}, bf16[256,1024]{1,0:T(8,128)(2,1)}, u32[]{:S(2)}) copy-start(bf16[256,1024]{1,0:T(8,128)(2,1)} %param.29) | copy-start | bytes 1572868
  309.7 96.5 %all-gather.17.cloned.1.call-start = ((), (), s32[]{:S(2)}) async-start(), calls=%async_computation.16 | async-start | bytes 2621440 | tf_op jit(solution)/shard_map/all_gather | solution.py:216
  383.5 6.4 copy-start.39
  383.5 94.5 %reduce-scatter.21.cloned.1.call-start = ((), (), s32[]{:S(2)}) async-start(), calls=%async_computation.20 | async-start | bytes 2359296 | tf_op jit(solution)/shard_map/reduce_scatter | solution.py:282
  389.9 159.2 %reduce-scatter.23.cloned.1.call-start = ((), (), s32[]{:S(2)}) async-start(), calls=%async_computation.21 | async-start | bytes 2359296 | tf_op jit(solution)/shard_map/reduce_scatter | solution.py:285
  396.6 218.0 %reduce-scatter.19.cloned.1.call-start = ((), (), s32[]{:S(2)}) async-start(), calls=%async_computation.19 | async-start | bytes 589824 | tf_op jit(solution)/shard_map/reduce_scatter | solution.py:279
  409.5 274.0 %reduce-scatter.17.cloned.1.call-start = ((), (), s32[]{:S(2)}) async-start(), calls=%async_computation.18 | async-start | bytes 1769472 | tf_op jit(solution)/shard_map/reduce_scatter | solution.py:276
  423.6 1.1 copy-start.3
  427.0 1.1 copy-start.12
  428.1 0.8 copy-start.13
  439.8 1.0 copy-start.3
  443.3 1.1 copy-start.12
  444.4 0.8 copy-start.13
  451.7 5.0 copy-start.26
  451.7 6.3 copy-start.27
  451.7 6.9 copy-start.21
  451.8 7.5 copy-start.5
  451.8 8.2 %copy-start.38 = (f32[1024]{0:T(1024)S(1)}, f32[1024]{0:T(1024)}, u32[]{:S(2)}) copy-start(f32[1024]{0:T(1024)} %get-tuple-element.321) | copy-start | bytes 12292
  451.8 26.3 %copy-start.18 = (f32[128,1024]{1,0:T(8,128)S(1)}, f32[128,1024]{1,0:T(8,128)}, u32[]{:S(2)}) copy-start(f32[128,1024]{1,0:T(8,128)} %param.39) | copy-start | bytes 1572868
  451.8 264.0 %reduce-scatter.15.cloned.1.call-start = ((), (), s32[]{:S(2)}) async-start(), calls=%async_computation.17 | async-start | bytes 2621440 | tf_op jit(solution)/shard_map/reduce_scatter | solution.py:263
  456.7 92.4 %copy-start.19 = (f32[128,1024]{1,0:T(8,128)S(1)}, f32[128,1024]{1,0:T(8,128)}, u32[]{:S(2)}) copy-start(f32[128,1024]{1,0:T(8,128)} %param.42) | copy-start | bytes 1572868
  456.7 92.4 %copy-start.20 = (f32[128,1024]{1,0:T(8,128)S(1)}, f32[128,1024]{1,0:T(8,128)}, u32[]{:S(2)}) copy-start(f32[128,1024]{1,0:T(8,128)} %param.41) | copy-start | bytes 1572868
  456.7 95.4 %copy-start.14 = (bf16[2,512,256]{1,2,0:T(8,128)(2,1)S(1)}, bf16[2,512,256]{1,2,0:T(8,128)(2,1)}, u32[]{:S(2)}) copy-start(bf16[2,512,256]{1,2,0:T(8,128)(2,1)} %get-tuple-element.150) | copy-start | bytes 1572868
  456.7 158.0 %copy-start.22 = (f32[128,256]{1,0:T(8,128)S(1)}, f32[128,256]{1,0:T(8,128)}, u32[]{:S(2)}) copy-start(f32[128,256]{1,0:T(8,128)} %param.36) | copy-start | bytes 393220
  456.7 158.0 %copy-start.23 = (f32[128,256]{1,0:T(8,128)S(1)}, f32[128,256]{1,0:T(8,128)}, u32[]{:S(2)}) copy-start(f32[128,256]{1,0:T(8,128)} %param.35) | copy-start | bytes 393220
  460.2 156.6 %copy-start.30 = (f32[4096]{0:T(1024)}, f32[4096]{0:T(1024)S(1)}, u32[]{:S(2)}) copy-start(f32[4096]{0:T(1024)S(1)} %dynamic_update_slice.40) | copy-start | bytes 49156
  460.2 255.6 %copy-start.2 = (bf16[256,1024]{1,0:T(8,128)(2,1)S(1)}, bf16[256,1024]{1,0:T(8,128)(2,1)}, u32[]{:S(2)}) copy-start(bf16[256,1024]{1,0:T(8,128)(2,1)} %param.28) | copy-start | bytes 1572868
  551.9 237.7 %copy-start.8 = (f32[128,1024]{1,0:T(8,128)S(1)}, f32[128,1024]{1,0:T(8,128)}, u32[]{:S(2)}) copy-start(f32[128,1024]{1,0:T(8,128)} %param.40) | copy-start | bytes 1572868
  553.3 63.5 %copy-start.33 = (f32[1,1024]{1,0:T(1,128)}, f32[1,1024]{1,0:T(1,128)S(1)}, u32[]{:S(2)}) copy-start(f32[1,1024]{1,0:T(1,128)S(1)} %constant_dynamic-update-slice_fusion.1) | copy-start | bytes 12292
  616.8 175.1 %copy-start.17 = (f32[128,256]{1,0:T(8,128)}, f32[128,256]{1,0:T(8,128)S(1)}, u32[]{:S(2)}) copy-start(f32[128,256]{1,0:T(8,128)S(1)} %get-tuple-element.275) | copy-start | bytes 393220
  616.8 175.1 %copy-start.10 = (f32[128,1024]{1,0:T(8,128)S(1)}, f32[128,1024]{1,0:T(8,128)}, u32[]{:S(2)}) copy-start(f32[128,1024]{1,0:T(8,128)} %param.37) | copy-start | bytes 1572868
  686.3 107.9 %copy-start.15 = (f32[128,3,256]{2,0,1:T(8,128)}, f32[128,3,256]{2,0,1:T(8,128)S(1)}, u32[]{:S(2)}) copy-start(f32[128,3,256]{2,0,1:T(8,128)S(1)} %get-tuple-element.279) | copy-start | bytes 1179652
  718.0 76.2 %copy-start.4 = (f32[256,1024]{1,0:T(8,128)S(1)}, f32[256,1024]{1,0:T(8,128)}, u32[]{:S(2)}) copy-start(f32[256,1024]{1,0:T(8,128)} %get-tuple-element.284) | copy-start | bytes 3145732
  781.5 12.8 %copy-start.29 = (f32[1,1024]{1,0:T(1,128)S(1)}, f32[1,1024]{1,0:T(1,128)}, u32[]{:S(2)}) copy-start(f32[1,1024]{1,0:T(1,128)} %copy-done.28) | copy-start | bytes 12292
  781.5 12.8 %copy-start.32 = (f32[256]{0:T(256)S(1)}, f32[256]{0:T(256)}, u32[]{:S(2)}) copy-start(f32[256]{0:T(256)} %copy-done.31) | copy-start | bytes 3076
  781.5 12.8 %copy-start.35 = (f32[256]{0:T(256)S(1)}, f32[256]{0:T(256)}, u32[]{:S(2)}) copy-start(f32[256]{0:T(256)} %copy-done.34) | copy-start | bytes 3076
  781.5 12.8 %copy-start.36 = (f32[256]{0:T(256)S(1)}, f32[256]{0:T(256)}, u32[]{:S(2)}) copy-start(f32[256]{0:T(256)} %broadcast_multiply_fusion) | copy-start | bytes 3076
  781.5 12.8 %copy-start.37 = (f32[256]{0:T(256)S(1)}, f32[256]{0:T(256)}, u32[]{:S(2)}) copy-start(f32[256]{0:T(256)} %broadcast_multiply_fusion.1) | copy-start | bytes 3076
  782.5 14.3 %copy-start.24 = (f32[6,1024]{1,0:T(8,128)}, f32[6,1024]{1,0:T(8,128)S(1)}, u32[]{:S(2)}) copy-start(f32[6,1024]{1,0:T(8,128)S(1)} %get-tuple-element.260) | copy-start | bytes 73732
  782.5 14.3 %copy-start.25 = (f32[6,1024]{1,0:T(8,128)}, f32[6,1024]{1,0:T(8,128)S(1)}, u32[]{:S(2)}) copy-start(f32[6,1024]{1,0:T(8,128)S(1)} %get-tuple-element.261) | copy-start | bytes 73732
Sparse Core Ops, SparseCore 0:
  10.6 51.4 all-gather.8
  64.3 20.3 all-gather.6
  117.7 44.5 reduce-scatter.8
  164.9 49.1 all-gather.10
  215.4 21.0 all-gather.14
  239.1 49.0 all-gather.12
  302.7 43.1 reduce-scatter.12
  348.4 31.1 reduce-scatter.10
  383.6 22.5 all-gather.16
  409.6 68.4 reduce-scatter.20
  481.6 67.4 reduce-scatter.22
  552.9 61.7 reduce-scatter.18
  618.1 65.3 reduce-scatter.16
  685.8 29.9 reduce-scatter.14
